TPU v7x, 32 devices: a whole 2x2x4 slice. The times are simulated.
32 devices in a mesh: seg: 4 (over z), grp: 4 (over y, x), pair: 2 (over core).
Axes of the slice: x: 2, y: 2, z: 4, core: 2. Of those that a mesh axis runs over, the one named last changes fastest.
Arguments:
- observations: float32 [128, 256], P(('grp', 'seg')), may hold values from -6 to 6
- masks: int32 [128, 256], P(('grp', 'seg')), may hold values 0 or 1
- gains: float32 [256], replicated, may hold values from 0.05 to 0.5
- transition: float32 [256, 256], replicated, may hold values from -1 to 1, as said below
- smoother_scale: float32 [256], replicated, may hold values from 0.995 to 0.9999
- initial_mean: float32 [256], replicated, may hold values from -8 to 8
Outputs:
- filtered: float32 [128, 256], P(('grp', 'seg'), 'pair')
- smoothed: float32 [128, 256], P(('grp', 'seg'), 'pair')
Inputs may be any that keep to these rules, and one draw needn't show every extreme that they name: Each column of transition is a unit vector scaled by a factor in (0, 1); the columns are orthogonal.
All inputs are finite; a program needn't handle non-finite values. No bound on the sum of `masks` on one device may be relied on, other than what follows from the above.
Results may differ from a plain program's by a relative error of at most 0.0003.
Values sent between devices are 32-bit elements; how exact they have to be, the bound alone decides.
No kernel may reach another device: no remote copies, remote signals or barrier semaphores. Data moves between devices by JAX's collectives and lax.ppermute only.
A program may use at most 64 MiB of HBM per device.

v0:
```python
import jax
import jax.numpy as jnp
from jax import lax
from jax.sharding import PartitionSpec as P


def entering(x, axis, combine, identity, reverse):
    size, here = (lax.axis_size(axis), lax.axis_index(axis))
    everything = jax.tree.map(lambda part: lax.all_gather(part, axis), x)
    start = jax.tree.map(
        lambda part, zero: jnp.broadcast_to(jnp.asarray(zero, part.dtype), part.shape), x, identity
    )

    def turn(k, before):
        at = size - 1 - k if reverse else k
        reached = at > here if reverse else at < here
        new = combine(before, jax.tree.map(lambda part: part[at], everything))
        return jax.tree.map(lambda a, b: jnp.where(reached, a, b), new, before)

    return lax.fori_loop(0, size, turn, start)


def spread(value, axis, source):
    kept = jnp.where(lax.axis_index(axis) == source, value, 0).astype(value.dtype)
    return lax.psum(kept, axis)


def shifted(value, axis, steps):
    count = lax.axis_size(axis)
    initial, last = (max(0, -steps), min(count, count - steps))
    return lax.ppermute(value, axis, [(source, source + steps) for source in range(initial, last)])


def compose(earlier, later_elem):
    highest = lax.Precision.HIGHEST
    matrix = jnp.dot(later_elem[0], earlier[0], precision=highest)
    offset = jnp.dot(later_elem[0], earlier[1], precision=highest) + later_elem[1]
    return (matrix, offset)


def shards(observations, masks, gains, transition, smoother_scale, initial_mean):
    highest = lax.Precision.HIGHEST
    state_width = transition.shape[0]
    day_count = observations.shape[0]
    observed = masks.astype(jnp.float32) * gains[None, :]
    retain = 1.0 - observed
    forcing = observed * observations
    smoother_gain = smoother_scale[:, None] * transition.T
    half_cols = state_width // lax.axis_size("pair")
    col_start = lax.axis_index("pair") * half_cols

    def forward_advance(position, product):
        scaled = jnp.dot(transition, product, precision=highest)
        return lax.dynamic_index_in_dim(retain, position, 0, False)[:, None] * scaled

    forward_half = lax.fori_loop(
        1,
        day_count,
        forward_advance,
        retain[0][:, None] * lax.dynamic_slice_in_dim(transition, col_start, half_cols, 1),
    )

    def gain_advance(position, product):
        return jnp.dot(smoother_gain, product, precision=highest)

    power_half = lax.fori_loop(
        1, day_count, gain_advance, lax.dynamic_slice_in_dim(smoother_gain, col_start, half_cols, 1)
    )
    fwd_matrix, gain_matrix = (
        lax.all_gather(forward_half, "pair", axis=1, tiled=True),
        lax.all_gather(power_half, "pair", axis=1, tiled=True),
    )

    def forward_run(mean_start):

        def forward_step(mean_prev, row_pair):
            retain_row, forcing_row = row_pair
            mean_next = retain_row * jnp.dot(transition, mean_prev, precision=highest) + forcing_row
            return (mean_next, mean_next)

        return lax.scan(forward_step, mean_start, (retain, forcing))

    def backward_run(smooth_end, means):

        def backward_step(smooth_next, mean_here):
            predicted = jnp.dot(transition, mean_here, precision=highest)
            smooth_here = mean_here + jnp.dot(
                smoother_gain, smooth_next - predicted, precision=highest
            )
            return (smooth_here, smooth_here)

        return lax.scan(backward_step, smooth_end, means, reverse=True)

    zeros_vec = jnp.zeros((state_width,), jnp.float32)
    identity = (jnp.eye(state_width, dtype=jnp.float32), zeros_vec)
    seg_count = lax.axis_size("seg")
    seg_index = lax.axis_index("seg")
    grp_count = lax.axis_size("grp")
    grp_index = lax.axis_index("grp")
    fwd_offset, unused = forward_run(zeros_vec)
    own_forward = (fwd_matrix, fwd_offset)
    before = entering(own_forward, "seg", compose, identity, False)
    through = compose(before, own_forward)
    group_total = (
        spread(through[0], "seg", seg_count - 1),
        spread(through[1], "seg", seg_count - 1),
    )
    entry_mean = initial_mean
    for rounds in range(1, grp_count):
        leaving = jnp.dot(group_total[0], entry_mean, precision=highest) + group_total[1]
        arrived = shifted(leaving, "grp", 1)
        entry_mean = jnp.where(grp_index == rounds, arrived, entry_mean)
    start_mean = jnp.dot(before[0], entry_mean, precision=highest) + before[1]
    last_mean, filtered = forward_run(start_mean)
    back_offset, unused_two = backward_run(zeros_vec, filtered)
    is_last = jnp.logical_and(seg_index == seg_count - 1, grp_index == grp_count - 1)
    boundary = jnp.dot(transition, last_mean, precision=highest)
    own_backward = (
        jnp.where(is_last, 0.0, gain_matrix),
        jnp.where(
            is_last, jnp.dot(gain_matrix, boundary, precision=highest) + back_offset, back_offset
        ),
    )
    behind = entering(own_backward, "seg", compose, identity, True)
    through_back = compose(behind, own_backward)
    back_total = (spread(through_back[0], "seg", 0), spread(through_back[1], "seg", 0))
    exit_smooth = zeros_vec
    for rounds in range(1, grp_count):
        leaving_back = jnp.dot(back_total[0], exit_smooth, precision=highest) + back_total[1]
        arrived_back = shifted(leaving_back, "grp", -1)
        exit_smooth = jnp.where(grp_index == grp_count - 1 - rounds, arrived_back, exit_smooth)
    smooth_end = jnp.dot(behind[0], exit_smooth, precision=highest) + behind[1]
    smooth_end = jnp.where(is_last, boundary, smooth_end)
    unused_three, smoothed = backward_run(smooth_end, filtered)
    out_cols = state_width // lax.axis_size("pair")
    out_start = lax.axis_index("pair") * out_cols
    filtered_part = lax.dynamic_slice_in_dim(filtered, out_start, out_cols, 1)
    smoothed_part = lax.dynamic_slice_in_dim(smoothed, out_start, out_cols, 1)
    return (filtered_part, smoothed_part)


def solution(mesh):
    return jax.shard_map(
        shards,
        mesh=mesh,
        in_specs=(P(("grp", "seg"), None), P(("grp", "seg"), None), P(), P(), P(), P()),
        out_specs=(P(("grp", "seg"), "pair"), P(("grp", "seg"), "pair")),
        check_vma=False,
    )
```

profile of v0, /device:TPU:0, one launch (start us, length us, event | category | flops | bytes accessed | tf_op | source)
XLA Modules:
  0.0 218.8 jit_solution(14768913008447524611)
XLA Ops:
  9.6 3.1 %while.113 = (s32[]{:T(128)}, f32[256,128]{1,0:T(8,128)S(1)}, f32[8,256]{1,0:T(8,128)S(1)}, f32[256,256]{1,0:T(8,128)S(1)}, s32[]{:T(128)}, /*index=5*/s32[]{:T(128)}, s32[]{:T(128)}) while((s32[]{:T(128)}, f32[256,128]{1,0:T(8,128)S(1)}, f32[8,256]{1,0:T(8,128)S(1)}, f32[256,256]{1,0:T(8,128)S(1)}, s32[]{:T(128)}, /*index=5*/s32[]{:T(128)}, ...), condition=%wide.region_1.2_spmd, body=%wide.region_0.1_spmd.sunk | while | flops 100696064 | bytes 789627 | solution.py:56
  12.7 2.3 %all_gather.30 = f32[256,256]{1,0:T(8,128)} all-gather(f32[256,128]{1,0:T(8,128)S(1)} %get-tuple-element.679), channel_id=1, replica_groups=mesh['seg'=4,'grp'=4,'pair'=2] {'pair'}, dimensions={1}, use_global_device_ids=true | all-gather | bytes 393216 | tf_op jit(solution)/shard_map/all_gather | solution.py:70
  15.0 2.9 %while.117 = (s32[]{:T(128)}, f32[256]{0:T(256)S(1)}, f32[8,256]{1,0:T(8,128)S(1)}, f32[256,256]{1,0:T(8,128)S(1)}, f32[8,256]{1,0:T(8,128)S(1)}, /*index=5*/s32[]{:T(128)}, s32[]{:T(128)}) while((s32[]{:T(128)}, f32[256]{0:T(256)S(1)}, f32[8,256]{1,0:T(8,128)S(1)}, f32[256,256]{1,0:T(8,128)S(1)}, f32[8,256]{1,0:T(8,128)S(1)}, ...), condition=%wide.region_3.4_spmd.clone, body=%wide.region_2.3_spmd.clone.sunk | while | flops 787203 | bytes 274523 | solution.py:81
  18.0 12.5 %all-gather.4 = f32[4,1,256]{2,1,0:T(1,128)S(1)} all-gather(f32[1,1,256]{2,1,0:T(1,128)S(1)} %bitcast.253), channel_id=3, replica_groups=mesh['seg'=4,'grp'=4,'pair'=2] {'seg'}, dimensions={0}, use_global_device_ids=true | all-gather | bytes 5120 | tf_op jit(solution)/shard_map/all_gather | solution.py:9
  32.2 13.5 %all-gather.9.cloned.1.call-done = f32[1024,256]{1,0:T(8,128)} async-done(((f32[256,256]{1,0:T(8,128)}), f32[1024,256]{1,0:T(8,128)}) %all-gather.9.cloned.1.call-update) | async-done | bytes 1048592 | tf_op jit(solution)/shard_map/all_gather | solution.py:9
  45.7 10.8 %while.118 = (s32[]{:T(128)}, f32[256,256]{1,0:T(8,128)S(1)}, f32[256]{0:T(256)S(1)}, s32[]{:T(128)}, f32[4,256,256]{2,1,0:T(8,128)}, /*index=5*/f32[4,256]{1,0:T(4,128)S(1)}, s32[]{:T(128)}, s32[]{:T(128)}) while((s32[]{:T(128)}, f32[256,256]{1,0:T(8,128)S(1)}, f32[256]{0:T(256)S(1)}, s32[]{:T(128)}, f32[4,256,256]{2,1,0:T(8,128)}, ...), condition=%wide.region_5.6_spmd.clone, body=%wide.region_4.5_spmd.clone.sunk | while | flops 202179584 | bytes 1846383 | solution.py:20
  58.1 10.2 %psum.29 = f32[256]{0:T(256)S(1)} all-reduce(f32[256]{0:T(256)S(1)} %add_select_fusion.5), channel_id=1, replica_groups=mesh['seg'=4,'grp'=4,'pair'=2] {'seg'}, use_global_device_ids=true, to_apply=%region_7.8 | all-reduce | flops 256 | bytes 2048 | tf_op jit(solution)/shard_map/psum | solution.py:25
  68.3 24.4 %all-reduce.3.cloned.1.call-done = f32[256,256]{1,0:T(8,128)} async-done(((f32[256,256]{1,0:T(8,128)}), f32[256,256]{1,0:T(8,128)}) %all-reduce.3.cloned.1.call-update) | async-done | bytes 262160 | tf_op jit(solution)/shard_map/psum | solution.py:25
  94.0 3.4 %collective-permute-start = (f32[256]{0:T(256)S(1)}, f32[256]{0:T(256)S(1)}, u32[]{:S(2)}, u32[]{:S(2)}) collective-permute-start(f32[256]{0:T(256)S(1)} %add.218), channel_id=1, source_target_pairs={{0,2},{2,4},{4,6},{1,3},{3,5},{5,7},{8,10},{10,12},{12,14},{9,11},... | collective-permute-start | bytes 3080 | tf_op jit(solution)/shard_map/ppermute | solution.py:31
  97.4 2.9 %while.115 = (s32[]{:T(128)}, f32[256,128]{1,0:T(8,128)S(1)}, f32[256,256]{1,0:T(8,128)S(1)}, s32[]{:T(128)}) while((s32[]{:T(128)}, f32[256,128]{1,0:T(8,128)S(1)}, f32[256,256]{1,0:T(8,128)S(1)}, s32[]{:T(128)}) %tuple.227), condition=%wide.region_11.12_spmd, body=%wide.region_10.11_spmd.sunk | while | flops 100663296 | bytes 786485 | solution.py:66
  100.6 3.4 %collective-permute-start.1 = (f32[256]{0:T(256)S(1)}, f32[256]{0:T(256)S(1)}, u32[]{:S(2)}, u32[]{:S(2)}) collective-permute-start(f32[256]{0:T(256)S(1)} %add.219), channel_id=1, source_target_pairs={{0,2},{2,4},{4,6},{1,3},{3,5},{5,7},{8,10},{10,12},{12,14},{9,11},... | collective-permute-start | bytes 3080 | tf_op jit(solution)/shard_map/ppermute | solution.py:31
  104.1 2.0 all_gather.35
  106.3 3.5 %collective-permute-start.2 = (f32[256]{0:T(256)S(1)}, f32[256]{0:T(256)S(1)}, u32[]{:S(2)}, u32[]{:S(2)}) collective-permute-start(f32[256]{0:T(256)S(1)} %add.220), channel_id=1, source_target_pairs={{0,2},{2,4},{4,6},{1,3},{3,5},{5,7},{8,10},{10,12},{12,14},{9,11},... | collective-permute-start | bytes 3080 | tf_op jit(solution)/shard_map/ppermute | solution.py:31
  111.5 3.2 %while.114 = (s32[]{:T(128)}, f32[256]{0:T(256)S(1)}, f32[8,256]{1,0:T(8,128)S(1)}, f32[8,256]{1,0:T(8,128)S(1)}, f32[256,256]{1,0:T(8,128)S(1)}, /*index=5*/f32[8,256]{1,0:T(8,128)S(1)}, s32[]{:T(128)}, s32[]{:T(128)}) while((s32[]{:T(128)}, f32[256]{0:T(256)S(1)}, f32[8,256]{1,0:T(8,128)S(1)}, f32[8,256]{1,0:T(8,128)S(1)}, ...), condition=%wide.region_9.10_spmd, body=%wide.region_8.9_spmd.sunk | while | flops 786946 | bytes 274525 | solution.py:81
  114.7 5.3 %while.119 = (s32[]{:T(128)}, f32[256]{0:T(256)S(1)}, f32[8,256]{1,0:T(8,128)S(1)}, f32[256,256]{1,0:T(8,128)S(1)}, f32[256,256]{1,0:T(8,128)S(1)}, /*index=5*/s32[]{:T(128)}, s32[]{:T(128)}, s32[]{:T(128)}) while((s32[]{:T(128)}, f32[256]{0:T(256)S(1)}, f32[8,256]{1,0:T(8,128)S(1)}, f32[256,256]{1,0:T(8,128)S(1)}, ...), condition=%wide.region_13.14_spmd.clone, body=%wide.region_12.13_spmd.clone.sunk | while | flops 1573636 | bytes 536687 | solution.py:92
  120.7 10.2 %all-gather.5 = f32[4,1,256]{2,1,0:T(1,128)S(1)} all-gather(f32[1,1,256]{2,1,0:T(1,128)S(1)} %bitcast.260), channel_id=5, replica_groups=mesh['seg'=4,'grp'=4,'pair'=2] {'seg'}, dimensions={0}, use_global_device_ids=true | all-gather | bytes 5120 | tf_op jit(solution)/shard_map/all_gather | solution.py:9
  130.9 7.8 %all-gather.11.cloned.1.call-done = f32[1024,256]{1,0:T(8,128)} async-done(((f32[256,256]{1,0:T(8,128)}), f32[1024,256]{1,0:T(8,128)}) %all-gather.11.cloned.1.call-update) | async-done | bytes 1048592 | tf_op jit(solution)/shard_map/all_gather | solution.py:9
  138.7 10.9 %while.120 = (s32[]{:T(128)}, f32[256,256]{1,0:T(8,128)S(1)}, f32[256]{0:T(256)S(1)}, s32[]{:T(128)}, f32[4,256,256]{2,1,0:T(8,128)}, /*index=5*/f32[4,256]{1,0:...) while((s32[]{:T(128)}, f32[256,256]{1,0:T(8,128)S(1)}, f32[256]{0:T(256)S(1)}, ...), condition=%wide.region_15.16_spmd.clone, body=%wide.region_14.15_spmd.clone.sunk | while | flops 202179584 | bytes 1845429 | solution.py:20
  151.1 10.2 %psum.31 = f32[256]{0:T(256)S(1)} all-reduce(f32[256]{0:T(256)S(1)} %add_select_fusion.4), channel_id=1, replica_groups=mesh['seg'=4,'grp'=4,'pair'=2] {'seg'}, use_global_device_ids=true, to_apply=%region_17.18 | all-reduce | flops 256 | bytes 2048 | tf_op jit(solution)/shard_map/psum | solution.py:25
  161.3 24.7 %all-reduce.5.cloned.1.call-done = f32[256,256]{1,0:T(8,128)} async-done(((f32[256,256]{1,0:T(8,128)}), f32[256,256]{1,0:T(8,128)}) %all-reduce.5.cloned.1.call-update) | async-done | bytes 262160 | tf_op jit(solution)/shard_map/psum | solution.py:25
  188.6 4.2 %collective-permute-done.3 = f32[256]{0:T(256)S(1)} collective-permute-done((f32[256]{0:T(256)S(1)}, f32[256]{0:T(256)S(1)}, u32[]{:S(2)}, u32[]{:S(2)}) %collective-permute-start.3) | collective-permute-done | bytes 1056 | tf_op jit(solution)/shard_map/ppermute | solution.py:31
  194.4 4.5 %collective-permute-done.4 = f32[256]{0:T(256)S(1)} collective-permute-done((f32[256]{0:T(256)S(1)}, f32[256]{0:T(256)S(1)}, u32[]{:S(2)}, u32[]{:S(2)}) %collective-permute-start.4) | collective-permute-done | bytes 1056 | tf_op jit(solution)/shard_map/ppermute | solution.py:31
  200.5 5.1 %collective-permute-done.5 = f32[256]{0:T(256)S(1)} collective-permute-done((f32[256]{0:T(256)S(1)}, f32[256]{0:T(256)S(1)}, u32[]{:S(2)}, u32[]{:S(2)}) %collective-permute-start.5) | collective-permute-done | bytes 1056 | tf_op jit(solution)/shard_map/ppermute | solution.py:31
  205.9 5.8 %while.116 = (s32[]{:T(128)}, f32[256]{0:T(256)S(1)}, f32[8,256]{1,0:T(8,128)S(1)}, f32[8,256]{1,0:T(8,128)S(1)}, f32[256,256]{1,0:T(8,128)S(1)}, /*index=5*/f32...) while((s32[]{:T(128)}, f32[256]{0:T(256)S(1)}, f32[8,256]{1,0:T(8,128)S(1)}, f32[8,256]{1,0:T(8,128)S(1)}, ...), condition=%wide.region_19.20_spmd, body=%wide.region_18.19_spmd.sunk | while | flops 1573379 | bytes 538737 | solution.py:92
  (320 shorter events, 60.7 us)
Async XLA Ops:
  7.2 0.7 copy-start.8
  7.2 2.4 %copy-start = (f32[256,256]{1,0:T(8,128)S(1)}, f32[256,256]{1,0:T(8,128)}, u32[]{:S(2)}) copy-start(f32[256,256]{1,0:T(8,128)} %param.25) | copy-start | bytes 786436
  7.2 38.5 %all-gather.9.cloned.1.call-start = ((), (), s32[]{:S(2)}) async-start(), calls=%async_computation.2 | async-start | bytes 1310720 | tf_op jit(solution)/shard_map/all_gather | solution.py:9
  14.9 77.8 %all-reduce.3.cloned.1.call-start = ((), (), s32[]{:S(2)}) async-start(), calls=%async_computation | async-start | bytes 524288 | tf_op jit(solution)/shard_map/psum | solution.py:25
  30.6 0.7 copy-start.1
  31.3 0.7 copy-start.9
  32.1 13.6 %copy-start.3 = (f32[256,256]{1,0:T(8,128)S(1)}, f32[256,256]{1,0:T(8,128)}, u32[]{:S(2)}) copy-start(f32[256,256]{1,0:T(8,128)} %copy-done.1) | copy-start | bytes 786436
  45.7 10.9 %copy-start.5 = (f32[256,256]{1,0:T(8,128)S(1)}, f32[256,256]{1,0:T(8,128)}, u32[]{:S(2)}) copy-start(f32[256,256]{1,0:T(8,128)} %all_gather.30) | copy-start | bytes 786436
  57.7 81.0 %all-gather.11.cloned.1.call-start = ((), (), s32[]{:S(2)}) async-start(), calls=%async_computation.3 | async-start | bytes 1310720 | tf_op jit(solution)/shard_map/all_gather | solution.py:9
  68.3 24.4 %copy-start.10 = (f32[256]{0:T(256)S(1)}, f32[256]{0:T(256)}, u32[]{:S(2)}) copy-start(f32[256]{0:T(256)} %param.27) | copy-start | bytes 3076
  94.0 6.3 %collective-permute-start = (f32[256]{0:T(256)S(1)}, f32[256]{0:T(256)S(1)}, u32[]{:S(2)}, u32[]{:S(2)}) collective-permute-start(f32[256]{0:T(256)S(1)} %add.218), channel_id=1, source_target_pairs={{0,2},{2,4},{4,6},{1,3},{3,5},{5,7},{8,10},{10,12},{12,14},{9,11},... | collective-permute-start | bytes 3080 | tf_op jit(solution)/shard_map/ppermute | solution.py:31
  97.4 3.0 %copy-start.6 = (f32[256,256]{1,0:T(8,128)S(1)}, f32[256,256]{1,0:T(8,128)}, u32[]{:S(2)}) copy-start(f32[256,256]{1,0:T(8,128)} %all-reduce.3.cloned.1.call-done) | copy-start | bytes 786436
  100.6 5.4 %collective-permute-start.1 = (f32[256]{0:T(256)S(1)}, f32[256]{0:T(256)S(1)}, u32[]{:S(2)}, u32[]{:S(2)}) collective-permute-start(f32[256]{0:T(256)S(1)} %add.219), channel_id=1, source_target_pairs={{0,2},{2,4},{4,6},{1,3},{3,5},{5,7},{8,10},{10,12},{12,14},{9,11},... | collective-permute-start | bytes 3080 | tf_op jit(solution)/shard_map/ppermute | solution.py:31
  106.3 4.8 %collective-permute-start.2 = (f32[256]{0:T(256)S(1)}, f32[256]{0:T(256)S(1)}, u32[]{:S(2)}, u32[]{:S(2)}) collective-permute-start(f32[256]{0:T(256)S(1)} %add.220), channel_id=1, source_target_pairs={{0,2},{2,4},{4,6},{1,3},{3,5},{5,7},{8,10},{10,12},{12,14},{9,11},... | collective-permute-start | bytes 3080 | tf_op jit(solution)/shard_map/ppermute | solution.py:31
  110.6 75.3 %all-reduce.5.cloned.1.call-start = ((), (), s32[]{:S(2)}) async-start(), calls=%async_computation.1 | async-start | bytes 524288 | tf_op jit(solution)/shard_map/psum | solution.py:25
  120.0 18.7 %copy-start.2 = (f32[256,256]{1,0:T(8,128)S(1)}, f32[256,256]{1,0:T(8,128)}, u32[]{:S(2)}) copy-start(f32[256,256]{1,0:T(8,128)} %copy-done.1) | copy-start | bytes 786436
  138.7 10.9 %copy-start.4 = (f32[256,256]{1,0:T(8,128)S(1)}, f32[256,256]{1,0:T(8,128)}, u32[]{:S(2)}) copy-start(f32[256,256]{1,0:T(8,128)} %broadcast_select_fusion.3) | copy-start | bytes 786436
  185.9 6.8 %copy-start.7 = (f32[256,256]{1,0:T(8,128)S(1)}, f32[256,256]{1,0:T(8,128)}, u32[]{:S(2)}) copy-start(f32[256,256]{1,0:T(8,128)} %all-reduce.5.cloned.1.call-done) | copy-start | bytes 786436
  187.2 5.5 %collective-permute-start.3 = (f32[256]{0:T(256)S(1)}, f32[256]{0:T(256)S(1)}, u32[]{:S(2)}, u32[]{:S(2)}) collective-permute-start(f32[256]{0:T(256)S(1)} %add.224), channel_id=1, source_target_pairs={{2,0},{4,2},{6,4},{3,1},{5,3},{7,5},{10,8},{12,10},{14,12},{11,9},... | collective-permute-start | bytes 3080 | tf_op jit(solution)/shard_map/ppermute | solution.py:31
  193.0 5.9 %collective-permute-start.4 = (f32[256]{0:T(256)S(1)}, f32[256]{0:T(256)S(1)}, u32[]{:S(2)}, u32[]{:S(2)}) collective-permute-start(f32[256]{0:T(256)S(1)} %add.225), channel_id=1, source_target_pairs={{2,0},{4,2},{6,4},{3,1},{5,3},{7,5},{10,8},{12,10},{14,12},{11,9},... | collective-permute-start | bytes 3080 | tf_op jit(solution)/shard_map/ppermute | solution.py:31
  199.2 6.4 %collective-permute-start.5 = (f32[256]{0:T(256)S(1)}, f32[256]{0:T(256)S(1)}, u32[]{:S(2)}, u32[]{:S(2)}) collective-permute-start(f32[256]{0:T(256)S(1)} %add.226), channel_id=1, source_target_pairs={{2,0},{4,2},{6,4},{3,1},{5,3},{7,5},{10,8},{12,10},{14,12},{11,9},... | collective-permute-start | bytes 3080 | tf_op jit(solution)/shard_map/ppermute | solution.py:31
Sparse Core Ops, SparseCore 0:
  15.1 30.6 all-gather.8
  57.8 34.8 all-reduce.2
  110.7 27.9 all-gather.10
  150.8 35.0 all-reduce.4
where the time goes:
time: 220 us; the launch traced here: 219 us
  waiting for transfers between devices  84.6 us (38%)
  blocking collectives  47.4 us (22%)
  matrix products  46.8 us (21%)
  starting transfers between devices  14.5 us (7%)
  between operations  14.5 us (7%)
  local copies, waits for them, and re-layouts  5.48 us (2%)
  other arithmetic  3.67 us (2%)
    psum x2, waiting for transfers between devices, spread(): return lax.psum(kept, axis)  49 us
    all_gather x2, blocking collectives, entering(): everything = jax.tree.map(lambda part: lax.all_gather(part, axis), x)  22.7 us
    all_gather x2, waiting for transfers between devices, entering(): everything = jax.tree.map(lambda part: lax.all_gather(part, axis), x)  21.3 us
    psum x2, blocking collectives, spread(): return lax.psum(kept, axis)  20.5 us
    ppermute x6, starting transfers between devices, shifted(): lax.ppermute(value, axis, [(source, source + steps) for source in range(i...  14.3 us
    ppermute x6, waiting for transfers between devices, shifted(): lax.ppermute(value, axis, [(source, source + steps) for source in range(i...  14.2 us
    dot_general x10, matrix products, compose(): matrix = jnp.dot(later_elem[0], earlier[0], precision=highest)  12.9 us
    dot_general x10, matrix products, compose(): jnp.dot(later_elem[0], earlier[1], precision=highest) + later_elem[1]  10.4 us
  transfers between devices with their start and end apart: 10, of which 8 were waited for; matrix products, arithmetic and copies ran while one was open for 7% of the time, Pallas kernels for 0%

commit v1 on v0

--- a/solution.py
+++ b/solution.py
@@ -2,6 +2,8 @@
 import jax.numpy as jnp
 from jax import lax
 from jax.sharding import PartitionSpec as P
+
+skins_proceed = lambda x0, shard_axis: jnp.sum(lax.all_gather(x0, shard_axis), axis=0)
 
 
 def entering(x, axis, combine, identity, reverse):
@@ -22,7 +24,7 @@
 
 def spread(value, axis, source):
     kept = jnp.where(lax.axis_index(axis) == source, value, 0).astype(value.dtype)
-    return lax.psum(kept, axis)
+    return skins_proceed(kept, axis)
 
 
 def shifted(value, axis, steps):

time: 220 us -> 206 us (0.936)
  waiting for transfers between devices: 84.6 us -> 71.6 us
  other arithmetic: 3.67 us -> 6.35 us
    psum x2 -> x0, waiting for transfers between devices: 49 us -> none  [spread(): return lax.psum(kept, axis)]
    all_gather x0 -> x2, waiting for transfers between devices: none -> 34.5 us  [lax.all_gather(x0, shard_axis)]
    psum x2 -> x0, blocking collectives: 20.5 us -> none  [spread(): return lax.psum(kept, axis)]
    all_gather x0 -> x2, blocking collectives: none -> 18.9 us  [lax.all_gather(x0, shard_axis)]
    reduce_sum x0 -> x4, other arithmetic: none -> 2.68 us  [jnp.sum(lax.all_gather(x0, shard_axis), axis=0)]
  transfers between devices with their start and end apart: 10 -> 10, of which waited for: 8 -> 8; matrix products, arithmetic and copies ran while one was open for 7% -> 8% of each run, Pallas kernels for 0% -> 0%
where the time goes in v1:
time: 206 us; the launch traced here: 205 us
  waiting for transfers between devices  71.6 us (35%)
  blocking collectives  45.5 us (22%)
  matrix products  44.7 us (22%)
  starting transfers between devices  14.5 us (7%)
  between operations  14.4 us (7%)
  other arithmetic  6.35 us (3%)
  local copies, waits for them, and re-layouts  5.55 us (3%)
    all_gather x2, waiting for transfers between devices, lax.all_gather(x0, shard_axis)  34.5 us
    all_gather x2, waiting for transfers between devices, entering(): everything = jax.tree.map(lambda part: lax.all_gather(part, axis), x)  22.8 us
    all_gather x2, blocking collectives, entering(): everything = jax.tree.map(lambda part: lax.all_gather(part, axis), x)  22.3 us
    all_gather x2, blocking collectives, lax.all_gather(x0, shard_axis)  18.9 us
    ppermute x6, starting transfers between devices, shifted(): lax.ppermute(value, axis, [(source, source + steps) for source in range(i...  14.4 us
    ppermute x6, waiting for transfers between devices, shifted(): lax.ppermute(value, axis, [(source, source + steps) for source in range(i...  14.2 us
    dot_general x10, matrix products, compose(): matrix = jnp.dot(later_elem[0], earlier[0], precision=highest)  12.8 us
    dot_general x10, matrix products, compose(): jnp.dot(later_elem[0], earlier[1], precision=highest) + later_elem[1]  10.4 us
  transfers between devices with their start and end apart: 10, of which 8 were waited for; matrix products, arithmetic and copies ran while one was open for 8% of the time, Pallas kernels for 0%

profile of v1, /device:TPU:0, one launch (start us, length us, event | category | flops | bytes accessed | tf_op | source)
XLA Modules:
  0.0 204.6 jit_solution(11846632126981791315)
XLA Ops:
  9.6 3.1 %while.113 = (s32[]{:T(128)}, f32[256,128]{1,0:T(8,128)S(1)}, f32[8,256]{1,0:T(8,128)S(1)}, f32[256,256]{1,0:T(8,128)S(1)}, s32[]{:T(128)}, /*index=5*/s32[]{:T(128)}, s32[]{:T(128)}) while((s32[]{:T(128)}, f32[256,128]{1,0:T(8,128)S(1)}, f32[8,256]{1,0:T(8,128)S(1)}, f32[256,256]{1,0:T(8,128)S(1)}, s32[]{:T(128)}, /*index=5*/s32[]{:T(128)}, ...), condition=%wide.region_1.2_spmd, body=%wide.region_0.1_spmd.sunk | while | flops 100696064 | bytes 789627 | solution.py:58
  12.7 2.3 %all_gather.54 = f32[256,256]{1,0:T(8,128)} all-gather(f32[256,128]{1,0:T(8,128)S(1)} %get-tuple-element.679), channel_id=1, replica_groups=mesh['seg'=4,'grp'=4,'pair'=2] {'pair'}, dimensions={1}, use_global_device_ids=true | all-gather | bytes 393216 | tf_op jit(solution)/shard_map/all_gather | solution.py:72
  15.0 2.9 %while.117 = (s32[]{:T(128)}, f32[256]{0:T(256)S(1)}, f32[8,256]{1,0:T(8,128)S(1)}, f32[256,256]{1,0:T(8,128)S(1)}, f32[8,256]{1,0:T(8,128)S(1)}, /*index=5*/s32[]{:T(128)}, s32[]{:T(128)}) while((s32[]{:T(128)}, f32[256]{0:T(256)S(1)}, f32[8,256]{1,0:T(8,128)S(1)}, f32[256,256]{1,0:T(8,128)S(1)}, f32[8,256]{1,0:T(8,128)S(1)}, ...), condition=%wide.region_3.4_spmd.clone, body=%wide.region_2.3_spmd.clone.sunk | while | flops 787203 | bytes 274523 | solution.py:83
  17.9 12.6 %all-gather.8 = f32[4,1,256]{2,1,0:T(1,128)S(1)} all-gather(f32[1,1,256]{2,1,0:T(1,128)S(1)} %bitcast.259), channel_id=3, replica_groups=mesh['seg'=4,'grp'=4,'pair'=2] {'seg'}, dimensions={0}, use_global_device_ids=true | all-gather | bytes 5120 | tf_op jit(solution)/shard_map/all_gather | solution.py:11
  30.6 15.1 %all-gather.17.cloned.1.call-done = f32[1024,256]{1,0:T(8,128)} async-done(((f32[256,256]{1,0:T(8,128)}), f32[1024,256]{1,0:T(8,128)}) %all-gather.17.cloned.1.call-update) | async-done | bytes 1048592 | tf_op jit(solution)/shard_map/all_gather | solution.py:11
  45.7 10.8 %while.118 = (s32[]{:T(128)}, f32[256,256]{1,0:T(8,128)S(1)}, f32[256]{0:T(256)S(1)}, s32[]{:T(128)}, f32[4,256,256]{2,1,0:T(8,128)}, /*index=5*/f32[4,256]{1,0:T(4,128)S(1)}, s32[]{:T(128)}, s32[]{:T(128)}) while((s32[]{:T(128)}, f32[256,256]{1,0:T(8,128)S(1)}, f32[256]{0:T(256)S(1)}, s32[]{:T(128)}, f32[4,256,256]{2,1,0:T(8,128)}, ...), condition=%wide.region_5.6_spmd.clone, body=%wide.region_4.5_spmd.clone.sunk | while | flops 202179584 | bytes 1846383 | solution.py:22
  59.1 9.4 %all-gather.9 = f32[4,1,256]{2,1,0:T(1,128)S(1)} all-gather(f32[1,1,256]{2,1,0:T(1,128)S(1)} %bitcast.284), channel_id=5, replica_groups=mesh['seg'=4,'grp'=4,'pair'=2] {'seg'}, dimensions={0}, use_global_device_ids=true | all-gather | bytes 5120 | tf_op jit(solution)/shard_map/all_gather | solution.py:6
  68.5 16.7 %all-gather.19.cloned.1.call-done = f32[1024,256]{1,0:T(8,128)} async-done(((f32[256,256]{1,0:T(8,128)}), f32[1024,256]{1,0:T(8,128)}) %all-gather.19.cloned.1.call-update) | async-done | bytes 1048592 | tf_op jit(solution)/shard_map/all_gather | solution.py:6
  87.5 3.4 %collective-permute-start = (f32[256]{0:T(256)S(1)}, f32[256]{0:T(256)S(1)}, u32[]{:S(2)}, u32[]{:S(2)}) collective-permute-start(f32[256]{0:T(256)S(1)} %add.210), channel_id=1, source_target_pairs={{0,2},{2,4},{4,6},{1,3},{3,5},{5,7},{8,10},{10,12},{12,14},{9,11},... | collective-permute-start | bytes 3080 | tf_op jit(solution)/shard_map/ppermute | solution.py:33
  90.9 2.9 %while.115 = (s32[]{:T(128)}, f32[256,128]{1,0:T(8,128)S(1)}, f32[256,256]{1,0:T(8,128)S(1)}, s32[]{:T(128)}) while((s32[]{:T(128)}, f32[256,128]{1,0:T(8,128)S(1)}, f32[256,256]{1,0:T(8,128)S(1)}, s32[]{:T(128)}) %tuple.227), condition=%wide.region_11.12_spmd, body=%wide.region_10.11_spmd.sunk | while | flops 100663296 | bytes 786485 | solution.py:68
  94.2 3.4 %collective-permute-start.1 = (f32[256]{0:T(256)S(1)}, f32[256]{0:T(256)S(1)}, u32[]{:S(2)}, u32[]{:S(2)}) collective-permute-start(f32[256]{0:T(256)S(1)} %add.211), channel_id=1, source_target_pairs={{0,2},{2,4},{4,6},{1,3},{3,5},{5,7},{8,10},{10,12},{12,14},{9,11},... | collective-permute-start | bytes 3080 | tf_op jit(solution)/shard_map/ppermute | solution.py:33
  97.6 2.0 all_gather.63
  99.9 3.5 %collective-permute-start.2 = (f32[256]{0:T(256)S(1)}, f32[256]{0:T(256)S(1)}, u32[]{:S(2)}, u32[]{:S(2)}) collective-permute-start(f32[256]{0:T(256)S(1)} %add.212), channel_id=1, source_target_pairs={{0,2},{2,4},{4,6},{1,3},{3,5},{5,7},{8,10},{10,12},{12,14},{9,11},... | collective-permute-start | bytes 3080 | tf_op jit(solution)/shard_map/ppermute | solution.py:33
  105.0 3.2 %while.114 = (s32[]{:T(128)}, f32[256]{0:T(256)S(1)}, f32[8,256]{1,0:T(8,128)S(1)}, f32[8,256]{1,0:T(8,128)S(1)}, f32[256,256]{1,0:T(8,128)S(1)}, /*index=5*/f32[8,256]{1,0:T(8,128)S(1)}, s32[]{:T(128)}, s32[]{:T(128)}) while((s32[]{:T(128)}, f32[256]{0:T(256)S(1)}, f32[8,256]{1,0:T(8,128)S(1)}, f32[8,256]{1,0:T(8,128)S(1)}, ...), condition=%wide.region_9.10_spmd, body=%wide.region_8.9_spmd.sunk | while | flops 786946 | bytes 274525 | solution.py:83
  108.2 5.3 %while.119 = (s32[]{:T(128)}, f32[256]{0:T(256)S(1)}, f32[8,256]{1,0:T(8,128)S(1)}, f32[256,256]{1,0:T(8,128)S(1)}, f32[256,256]{1,0:T(8,128)S(1)}, /*index=5*/s32[]{:T(128)}, s32[]{:T(128)}, s32[]{:T(128)}) while((s32[]{:T(128)}, f32[256]{0:T(256)S(1)}, f32[8,256]{1,0:T(8,128)S(1)}, f32[256,256]{1,0:T(8,128)S(1)}, ...), condition=%wide.region_13.14_spmd.clone, body=%wide.region_12.13_spmd.clone.sunk | while | flops 1573636 | bytes 536687 | solution.py:94
  114.2 9.7 %all-gather.10 = f32[4,1,256]{2,1,0:T(1,128)S(1)} all-gather(f32[1,1,256]{2,1,0:T(1,128)S(1)} %bitcast.266), channel_id=7, replica_groups=mesh['seg'=4,'grp'=4,'pair'=2] {'seg'}, dimensions={0}, use_global_device_ids=true | all-gather | bytes 5120 | tf_op jit(solution)/shard_map/all_gather | solution.py:11
  123.9 7.7 %all-gather.21.cloned.1.call-done = f32[1024,256]{1,0:T(8,128)} async-done(((f32[256,256]{1,0:T(8,128)}), f32[1024,256]{1,0:T(8,128)}) %all-gather.21.cloned.1.call-update) | async-done | bytes 1048592 | tf_op jit(solution)/shard_map/all_gather | solution.py:11
  131.6 10.9 %while.120 = (s32[]{:T(128)}, f32[256,256]{1,0:T(8,128)S(1)}, f32[256]{0:T(256)S(1)}, s32[]{:T(128)}, f32[4,256,256]{2,1,0:T(8,128)}, /*index=5*/f32[4,256]{1,0:...) while((s32[]{:T(128)}, f32[256,256]{1,0:T(8,128)S(1)}, f32[256]{0:T(256)S(1)}, ...), condition=%wide.region_15.16_spmd.clone, body=%wide.region_14.15_spmd.clone.sunk | while | flops 202179584 | bytes 1845429 | solution.py:22
  144.0 9.5 %all-gather.11 = f32[4,1,256]{2,1,0:T(1,128)S(1)} all-gather(f32[1,1,256]{2,1,0:T(1,128)S(1)} %bitcast.283), channel_id=9, replica_groups=mesh['seg'=4,'grp'=4,'pair'=2] {'seg'}, dimensions={0}, use_global_device_ids=true | all-gather | bytes 5120 | tf_op jit(solution)/shard_map/all_gather | solution.py:6
  153.5 17.8 %all-gather.23.cloned.1.call-done = f32[1024,256]{1,0:T(8,128)} async-done(((f32[256,256]{1,0:T(8,128)}), f32[1024,256]{1,0:T(8,128)}) %all-gather.23.cloned.1.call-update) | async-done | bytes 1048592 | tf_op jit(solution)/shard_map/all_gather | solution.py:6
  174.3 4.2 %collective-permute-done.3 = f32[256]{0:T(256)S(1)} collective-permute-done((f32[256]{0:T(256)S(1)}, f32[256]{0:T(256)S(1)}, u32[]{:S(2)}, u32[]{:S(2)}) %collective-permute-start.3) | collective-permute-done | bytes 1056 | tf_op jit(solution)/shard_map/ppermute | solution.py:33
  180.1 4.5 %collective-permute-done.4 = f32[256]{0:T(256)S(1)} collective-permute-done((f32[256]{0:T(256)S(1)}, f32[256]{0:T(256)S(1)}, u32[]{:S(2)}, u32[]{:S(2)}) %collective-permute-start.4) | collective-permute-done | bytes 1056 | tf_op jit(solution)/shard_map/ppermute | solution.py:33
  186.2 5.1 %collective-permute-done.5 = f32[256]{0:T(256)S(1)} collective-permute-done((f32[256]{0:T(256)S(1)}, f32[256]{0:T(256)S(1)}, u32[]{:S(2)}, u32[]{:S(2)}) %collective-permute-start.5) | collective-permute-done | bytes 1056 | tf_op jit(solution)/shard_map/ppermute | solution.py:33
  191.6 5.8 %while.116 = (s32[]{:T(128)}, f32[256]{0:T(256)S(1)}, f32[8,256]{1,0:T(8,128)S(1)}, f32[8,256]{1,0:T(8,128)S(1)}, f32[256,256]{1,0:T(8,128)S(1)}, /*index=5*/f32...) while((s32[]{:T(128)}, f32[256]{0:T(256)S(1)}, f32[8,256]{1,0:T(8,128)S(1)}, f32[8,256]{1,0:T(8,128)S(1)}, ...), condition=%wide.region_19.20_spmd, body=%wide.region_18.19_spmd.sunk | while | flops 1573379 | bytes 538737 | solution.py:94
  (315 shorter events, 61.4 us)
Async XLA Ops:
  7.2 0.7 copy-start.3
  7.2 2.4 %copy-start = (f32[256,256]{1,0:T(8,128)S(1)}, f32[256,256]{1,0:T(8,128)}, u32[]{:S(2)}) copy-start(f32[256,256]{1,0:T(8,128)} %param.25) | copy-start | bytes 786436
  7.2 38.5 %all-gather.17.cloned.1.call-start = ((), (), s32[]{:S(2)}) async-start(), calls=%async_computation | async-start | bytes 1310720 | tf_op jit(solution)/shard_map/all_gather | solution.py:11
  14.9 70.3 %all-gather.19.cloned.1.call-start = ((), (), s32[]{:S(2)}) async-start(), calls=%async_computation.1 | async-start | bytes 1310720 | tf_op jit(solution)/shard_map/all_gather | solution.py:6
  45.7 10.8 %copy-start.2 = (f32[256,256]{1,0:T(8,128)S(1)}, f32[256,256]{1,0:T(8,128)}, u32[]{:S(2)}) copy-start(f32[256,256]{1,0:T(8,128)} %all_gather.54) | copy-start | bytes 786436
  57.7 73.9 %all-gather.21.cloned.1.call-start = ((), (), s32[]{:S(2)}) async-start(), calls=%async_computation.2 | async-start | bytes 1310720 | tf_op jit(solution)/shard_map/all_gather | solution.py:11
  57.9 0.7 copy-start.4
  86.6 0.7 copy-start.5
  87.5 6.3 %collective-permute-start = (f32[256]{0:T(256)S(1)}, f32[256]{0:T(256)S(1)}, u32[]{:S(2)}, u32[]{:S(2)}) collective-permute-start(f32[256]{0:T(256)S(1)} %add.210), channel_id=1, source_target_pairs={{0,2},{2,4},{4,6},{1,3},{3,5},{5,7},{8,10},{10,12},{12,14},{9,11},... | collective-permute-start | bytes 3080 | tf_op jit(solution)/shard_map/ppermute | solution.py:33
  94.2 5.4 %collective-permute-start.1 = (f32[256]{0:T(256)S(1)}, f32[256]{0:T(256)S(1)}, u32[]{:S(2)}, u32[]{:S(2)}) collective-permute-start(f32[256]{0:T(256)S(1)} %add.211), channel_id=1, source_target_pairs={{0,2},{2,4},{4,6},{1,3},{3,5},{5,7},{8,10},{10,12},{12,14},{9,11},... | collective-permute-start | bytes 3080 | tf_op jit(solution)/shard_map/ppermute | solution.py:33
  99.9 4.8 %collective-permute-start.2 = (f32[256]{0:T(256)S(1)}, f32[256]{0:T(256)S(1)}, u32[]{:S(2)}, u32[]{:S(2)}) collective-permute-start(f32[256]{0:T(256)S(1)} %add.212), channel_id=1, source_target_pairs={{0,2},{2,4},{4,6},{1,3},{3,5},{5,7},{8,10},{10,12},{12,14},{9,11},... | collective-permute-start | bytes 3080 | tf_op jit(solution)/shard_map/ppermute | solution.py:33
  104.1 67.2 %all-gather.23.cloned.1.call-start = ((), (), s32[]{:S(2)}) async-start(), calls=%async_computation.3 | async-start | bytes 1310720 | tf_op jit(solution)/shard_map/all_gather | solution.py:6
  131.6 10.9 %copy-start.1 = (f32[256,256]{1,0:T(8,128)S(1)}, f32[256,256]{1,0:T(8,128)}, u32[]{:S(2)}) copy-start(f32[256,256]{1,0:T(8,128)} %broadcast_select_fusion.3) | copy-start | bytes 786436
  172.9 5.5 %collective-permute-start.3 = (f32[256]{0:T(256)S(1)}, f32[256]{0:T(256)S(1)}, u32[]{:S(2)}, u32[]{:S(2)}) collective-permute-start(f32[256]{0:T(256)S(1)} %add.216), channel_id=1, source_target_pairs={{2,0},{4,2},{6,4},{3,1},{5,3},{7,5},{10,8},{12,10},{14,12},{11,9},... | collective-permute-start | bytes 3080 | tf_op jit(solution)/shard_map/ppermute | solution.py:33
  178.7 5.9 %collective-permute-start.4 = (f32[256]{0:T(256)S(1)}, f32[256]{0:T(256)S(1)}, u32[]{:S(2)}, u32[]{:S(2)}) collective-permute-start(f32[256]{0:T(256)S(1)} %add.217), channel_id=1, source_target_pairs={{2,0},{4,2},{6,4},{3,1},{5,3},{7,5},{10,8},{12,10},{14,12},{11,9},... | collective-permute-start | bytes 3080 | tf_op jit(solution)/shard_map/ppermute | solution.py:33
  184.9 6.4 %collective-permute-start.5 = (f32[256]{0:T(256)S(1)}, f32[256]{0:T(256)S(1)}, u32[]{:S(2)}, u32[]{:S(2)}) collective-permute-start(f32[256]{0:T(256)S(1)} %add.218), channel_id=1, source_target_pairs={{2,0},{4,2},{6,4},{3,1},{5,3},{7,5},{10,8},{12,10},{14,12},{11,9},... | collective-permute-start | bytes 3080 | tf_op jit(solution)/shard_map/ppermute | solution.py:33
Sparse Core Ops, SparseCore 0:
  15.1 30.6 all-gather.16
  57.8 27.3 all-gather.18
  104.3 27.3 all-gather.20
  143.8 27.5 all-gather.22
